TPU v7x, 512 devices: a whole 4x8x8 slice. The times are simulated.
512 devices in a mesh: dp: 16 (over z, x_lo), space: 32 (over y, x_hi, core).
Axes of the slice: x: 4 (x_hi: 2, x_lo: 2; x = x_hi * 2 + x_lo), y: 8, z: 8, core: 2. Of those that a mesh axis runs over, the one named last changes fastest.
Arguments:
- features: bfloat16 [16, 64, 72, 2048], P('dp', 'space'), may hold values from -150 to 150
- depthwise: bfloat16 [2, 9, 2048], replicated, may hold values from -2 to 2
- pointwise: bfloat16 [2048, 512], replicated, may hold values from -0.125 to 0.125
- bn_gain: float32 [2, 2048], replicated, may hold values from 0.1 to 1.9
- cotangent: bfloat16 [16, 64, 72, 256], P('dp', 'space'), may hold values from -6 to 6
Outputs:
- block_out: bfloat16 [16, 64, 72, 256], P('dp', 'space')
- grad_pointwise: float32 [2048, 512], P('space')
- grad_depthwise: float32 [2, 9, 2048], P(None, None, 'space')
All inputs are finite; a program needn't handle non-finite values.
Results may differ from a plain program's by a relative error of at most 0.001.
The roundings to bfloat16 on the way count: a program that leaves them out, or rounds other values in their place, can miss the bound.
Values may be sent and summed in bfloat16 or wider, within the bound.
No kernel may reach another device: no remote copies, remote signals or barrier semaphores. Data moves between devices by JAX's collectives and lax.ppermute only.
A program may use at most 64 MiB of HBM per device.

v0:
```python
import jax
import jax.numpy as jnp
from jax import lax
from jax.sharding import PartitionSpec as P

NEAR_DILATION = 12
FAR_DILATION = 24
eps_norm = 1e-05


def shifted(value, axis, steps):
    count = lax.axis_size(axis)
    leading, last = (max(0, -steps), min(count, count - steps))
    return lax.ppermute(value, axis, [(source, source + steps) for source in range(leading, last)])


def shift_dim(input_values, offset, reduce_axis):
    if offset == 0:
        return input_values
    extent = abs(offset)
    length_here = input_values.shape[reduce_axis]
    padding = [(0, 0)] * input_values.ndim
    padding[reduce_axis] = (extent, extent)
    padded = jnp.pad(input_values, padding)
    return lax.slice_in_dim(
        padded, extent + offset, extent + offset + length_here, axis=reduce_axis
    )


def depthwise_out(sources, weights, dilation, col_axis):
    running_total = jnp.zeros(sources[1].shape, jnp.float32)
    for row_tap in range(3):
        for col_tap in range(3):
            moved = shift_dim(sources[row_tap], (col_tap - 1) * dilation, col_axis)
            running_total = running_total + weights[3 * row_tap + col_tap].astype(
                jnp.float32
            ) * moved.astype(jnp.float32)
    return running_total


def depthwise_grad(sources, gradient_map, dilation, col_axis, sum_axes):
    results = []
    for row_tap in range(3):
        for col_tap in range(3):
            moved = shift_dim(sources[row_tap], (col_tap - 1) * dilation, col_axis)
            results.append(
                jnp.sum(gradient_map.astype(jnp.float32) * moved.astype(jnp.float32), axis=sum_axes)
            )
    return jnp.stack(results)


def remote_sources(features, dilation):
    row_count = features.shape[1]
    steps_away = dilation // row_count
    above = shifted(features, "space", steps_away)
    below = shifted(features, "space", -steps_away)
    return (above, features, below)


def body(features, depthwise, pointwise, bn_gain, cotangent):
    dilation_rates = (NEAR_DILATION, FAR_DILATION)
    row_count = features.shape[1]
    map_width = features.shape[2]
    channels = features.shape[3]
    out_width = pointwise.shape[1] // 2
    space_count = lax.axis_size("space")
    sample_count = lax.axis_size("dp")
    chan_share = channels // space_count
    position = lax.axis_index("space")
    pixels = row_count * map_width
    count = float(sample_count * space_count * row_count * map_width)
    sources = [remote_sources(features, dilation_rates[k]) for k in range(2)]
    branch_vals = jnp.stack(
        [depthwise_out(sources[k], depthwise[k], dilation_rates[k], 2) for k in range(2)]
    ).astype(jnp.bfloat16)
    input_values = branch_vals.astype(jnp.float32)
    sum_vals, sum_squares = lax.psum(
        (
            jnp.sum(input_values, axis=(1, 2, 3)),
            jnp.sum(input_values * input_values, axis=(1, 2, 3)),
        ),
        ("dp", "space"),
    )
    batch_average = sum_vals / count
    variance = sum_squares / count - batch_average * batch_average
    inverse_deviation = lax.rsqrt(variance + eps_norm)[:, None, None, None, :]
    norm_gains = bn_gain[:, None, None, None, :]
    normalized_input = (input_values - batch_average[:, None, None, None, :]) * inverse_deviation
    scaled_values = norm_gains * normalized_input
    used = jnp.maximum(scaled_values, 0.0).astype(jnp.bfloat16)
    flattened_used = used.reshape(2, pixels, channels)
    gradient_rows = cotangent.reshape(pixels, out_width)
    branch_output = jnp.dot(
        flattened_used[0], pointwise[:, :out_width], preferred_element_type=jnp.float32
    ) + jnp.dot(flattened_used[1], pointwise[:, out_width:], preferred_element_type=jnp.float32)
    block_out = branch_output.astype(jnp.bfloat16).reshape(1, row_count, map_width, out_width)
    pieces = []
    for branch_no in range(2):
        columns = flattened_used[branch_no]
        pieces.append(
            lax.dot_general(
                columns, gradient_rows, (((0,), (0,)), ((), ())), preferred_element_type=jnp.float32
            )
        )
    snapshot_grad = lax.psum_scatter(
        jnp.concatenate(pieces, axis=1), "space", scatter_dimension=0, tiled=True
    )
    grad_pw = lax.psum(snapshot_grad, "dp")
    grad_used = jnp.stack(
        [
            lax.dot_general(
                gradient_rows,
                pointwise[:, k * out_width : (k + 1) * out_width],
                (((1,), (1,)), ((), ())),
                preferred_element_type=jnp.float32,
            )
            for k in range(2)
        ]
    )
    grad_used = grad_used.reshape(2, 1, row_count, map_width, channels)
    normalized_gradient = jnp.where(scaled_values > 0, grad_used, 0.0) * norm_gains
    first_sums, second_sums = lax.psum(
        (
            jnp.sum(normalized_gradient, axis=(1, 2, 3)),
            jnp.sum(normalized_gradient * normalized_input, axis=(1, 2, 3)),
        ),
        ("dp", "space"),
    )
    mean_first_moment = (first_sums / count)[:, None, None, None, :]
    mean_second_moment = (second_sums / count)[:, None, None, None, :]
    gradient_values = (
        inverse_deviation
        * (normalized_gradient - mean_first_moment - normalized_input * mean_second_moment)
    ).astype(jnp.bfloat16)
    local_grads = jnp.stack(
        [
            depthwise_grad(sources[k], gradient_values[k], dilation_rates[k], 2, (0, 1, 2))
            for k in range(2)
        ]
    )
    summed = lax.psum(local_grads, ("dp", "space"))
    grad_dw = lax.dynamic_slice_in_dim(summed, position * chan_share, chan_share, 2)
    return (block_out, grad_pw, grad_dw)


def solution(mesh):
    in_specs = (P("dp", "space", None, None), P(), P(), P(), P("dp", "space", None, None))
    out_specs = (P("dp", "space", None, None), P("space", None), P(None, None, "space"))
    return jax.shard_map(body, mesh=mesh, in_specs=in_specs, out_specs=out_specs, check_vma=False)
```

profile of v0, /device:TPU:2, one launch (start us, length us, event | category | flops | bytes accessed | tf_op | source)
XLA Modules:
  0.0 725.3 jit_solution(8803910029780150236)
XLA Ops:
  8.1 5.7 collective-permute-start.2
  13.8 1.3 collective-permute-start.1
  15.1 7.0 collective-permute-start
  22.1 1.3 collective-permute-start.3
  23.4 1.7 convolution_bitcast_fusion
  25.2 0.5 convolution_bitcast_fusion.1
  25.7 7.6 %collective-permute-done.1 = bf16[1,2,72,2048]{3,2,1,0:T(8,128)(2,1)S(1)} collective-permute-done((bf16[1,2,72,2048]{3,2,1,0:T(8,128)(2,1)}, bf16[1,2,72,2048]{3,2,1,0:T(8,128)(2,1)S(1)}, u32[]{:S(2)}, u32[]{:S(2)}) %collective-permute-start.1) | collective-permute-done | bytes 589856 | tf_op jit(solution)/shard_map/ppermute | solution.py:14
  33.3 11.6 %collective-permute-done = bf16[1,2,72,2048]{3,2,1,0:T(8,128)(2,1)S(1)} collective-permute-done((bf16[1,2,72,2048]{3,2,1,0:T(8,128)(2,1)}, bf16[1,2,72,2048]{3,2,1,0:T(8,128)(2,1)S(1)}, u32[]{:S(2)}, u32[]{:S(2)}) %collective-permute-start) | collective-permute-done | bytes 589856 | tf_op jit(solution)/shard_map/ppermute | solution.py:14
  44.9 1.1 fusion.58
  46.1 25.9 %collective-permute-done.3 = bf16[1,2,72,2048]{3,2,1,0:T(8,128)(2,1)S(1)} collective-permute-done((bf16[1,2,72,2048]{3,2,1,0:T(8,128)(2,1)}, bf16[1,2,72,2048]{3,2,1,0:T(8,128)(2,1)S(1)}, u32[]{:S(2)}, u32[]{:S(2)}) %collective-permute-start.3) | collective-permute-done | bytes 589856 | tf_op jit(solution)/shard_map/ppermute | solution.py:14
  72.0 0.8 fusion.57
  72.9 0.8 copy-done.2
  74.1 121.6 %all-reduce.7 = (f32[2,2048]{1,0:T(2,128)S(1)}, f32[2,2048]{1,0:T(2,128)S(1)}) all-reduce(f32[2,2048]{1,0:T(2,128)S(1)} %get-tuple-element.42, f32[2,2048]{1,0:T(2,128)S(1)} %get-tuple-element.41), channel_id=1, replica_groups=mesh['dp'=16,'space'=32] {'dp','space'}, use_global_device_ids=true, to_apply=%region_3.4 | all-reduce | flops 8192 | bytes 65536 | tf_op jit(solution)/shard_map/psum | solution.py:77
  195.7 2.0 fusion.61
  197.7 93.1 %all-reduce.6 = (f32[2,2048]{1,0:T(2,128)S(1)}, f32[2,2048]{1,0:T(2,128)S(1)}) all-reduce(f32[2,2048]{1,0:T(2,128)S(1)} %get-tuple-element.13, f32[2,2048]{1,0:T(2,128)S(1)} %get-tuple-element.12), channel_id=1, replica_groups=mesh['dp'=16,'space'=32] {'dp','space'}, use_global_device_ids=true, to_apply=%region_9.10 | all-reduce | flops 8192 | bytes 65536 | tf_op jit(solution)/shard_map/psum | solution.py:122
  290.8 3.2 fusion.10
  294.1 0.5 fusion.64
  295.4 2.5 pad_maximum_fusion
  297.9 5.3 copy.13
  303.3 1.2 copy-done.1
  304.8 1.5 fusion.36
  306.4 1.4 fusion.39
  308.1 0.7 pad_maximum_fusion.2
  308.9 1.6 fusion.55
  310.5 121.4 %reduce-scatter.4.cloned.1.call-done = f32[64,512]{1,0:T(8,128)} async-done(((f32[2048,512]{1,0:T(8,128)}), f32[64,512]{1,0:T(8,128)}) %reduce-scatter.4.cloned.1.call-update) | async-done | bytes 131088
  431.9 1.7 copy.14
  433.7 2.2 fusion.49
  435.9 136.4 %all-reduce.13.cloned.1.call-done = f32[2,9,2048]{2,1,0:T(8,128)} async-done(((f32[2,9,2048]{2,1,0:T(8,128)}), f32[2,9,2048]{2,1,0:T(8,128)}) %all-reduce.13.cloned.1.call-update) | async-done | bytes 147472 | tf_op jit(solution)/shard_map/psum | solution.py:141
  572.3 0.8 constant_dynamic-slice_fusion
  573.1 0.6 copy.12
  573.7 142.5 %all-reduce.11.cloned.1.call-done = f32[64,512]{0,1:T(8,128)} async-done(((f32[64,512]{0,1:T(8,128)}), f32[64,512]{0,1:T(8,128)}) %all-reduce.11.cloned.1.call-update) | async-done | bytes 131088 | tf_op jit(solution)/shard_map/psum | solution.py:108
  716.2 1.7 copy.11
  (49 shorter events, 2.2 us)
Async XLA Ops:
  8.0 15.4 %copy-start = (bf16[1,2,72,256]{3,2,1,0:T(8,128)(2,1)S(1)}, bf16[1,2,72,256]{3,2,1,0:T(8,128)(2,1)}, u32[]{:S(2)}) copy-start(bf16[1,2,72,256]{3,2,1,0:T(8,128)(2,1)} %param.9) | copy-start | bytes 221188
  8.0 17.1 %copy-start.16 = (bf16[2,9,2048]{2,0,1:T(2,128)(2,1)S(1)}, bf16[2,9,2048]{2,0,1:T(2,128)(2,1)}, u32[]{:S(2)}) copy-start(bf16[2,9,2048]{2,0,1:T(2,128)(2,1)} %param.6) | copy-start | bytes 221188
  8.0 423.9 %reduce-scatter.4.cloned.1.call-start = ((), (), s32[]{:S(2)}) async-start(), calls=%async_computation.3 | async-start | bytes 4325376
  8.1 17.1 %copy-start.15 = (bf16[2048,512]{1,0:T(8,128)(2,1)S(1)}, bf16[2048,512]{1,0:T(8,128)(2,1)}, u32[]{:S(2)}) copy-start(bf16[2048,512]{1,0:T(8,128)(2,1)} %param.7) | copy-start | bytes 6291460
  8.1 38.0 %collective-permute-start.2 = (bf16[1,2,72,2048]{3,2,1,0:T(8,128)(2,1)}, bf16[1,2,72,2048]{3,2,1,0:T(8,128)(2,1)S(1)}, u32[]{:S(2)}, u32[]{:S(2)}) collective-permute-start(bf16[1,2,72,2048]{3,2,1,0:T(8,128)(2,1)} %param.5), channel_id=1, source_target_pairs={{0,12},{1,13},{2,14},{3,15},{4,16},{5,17},{6,18},{7,19},{8,20},{9,... | collective-permute-start | bytes 1769480 | tf_op jit(solution)/shard_map/ppermute | solution.py:14
  13.8 19.5 %collective-permute-start.1 = (bf16[1,2,72,2048]{3,2,1,0:T(8,128)(2,1)}, bf16[1,2,72,2048]{3,2,1,0:T(8,128)(2,1)S(1)}, u32[]{:S(2)}, u32[]{:S(2)}) collective-permute-start(bf16[1,2,72,2048]{3,2,1,0:T(8,128)(2,1)} %param.5), channel_id=1, source_target_pairs={{6,0},{7,1},{8,2},{9,3},{10,4},{11,5},{12,6},{13,7},{14,8},{15,9},... | collective-permute-start | bytes 1769480 | tf_op jit(solution)/shard_map/ppermute | solution.py:14
  15.1 29.8 %collective-permute-start = (bf16[1,2,72,2048]{3,2,1,0:T(8,128)(2,1)}, bf16[1,2,72,2048]{3,2,1,0:T(8,128)(2,1)S(1)}, u32[]{:S(2)}, u32[]{:S(2)}) collective-permute-start(bf16[1,2,72,2048]{3,2,1,0:T(8,128)(2,1)} %param.5), channel_id=1, source_target_pairs={{0,6},{1,7},{2,8},{3,9},{4,10},{5,11},{6,12},{7,13},{8,14},{9,15},... | collective-permute-start | bytes 1769480 | tf_op jit(solution)/shard_map/ppermute | solution.py:14
  22.1 50.0 %collective-permute-start.3 = (bf16[1,2,72,2048]{3,2,1,0:T(8,128)(2,1)}, bf16[1,2,72,2048]{3,2,1,0:T(8,128)(2,1)S(1)}, u32[]{:S(2)}, u32[]{:S(2)}) collective-permute-start(bf16[1,2,72,2048]{3,2,1,0:T(8,128)(2,1)} %param.5), channel_id=1, source_target_pairs={{12,0},{13,1},{14,2},{15,3},{16,4},{17,5},{18,6},{19,7},{20,8},{21... | collective-permute-start | bytes 1769480 | tf_op jit(solution)/shard_map/ppermute | solution.py:14
  25.2 19.7 %copy-start.3 = (bf16[1,2,72,2048]{3,2,1,0:T(8,128)(2,1)S(1)}, bf16[1,2,72,2048]{3,2,1,0:T(8,128)(2,1)}, u32[]{:S(2)}) copy-start(bf16[1,2,72,2048]{3,2,1,0:T(8,128)(2,1)} %param.5) | copy-start | bytes 1769476
  33.3 12.8 %copy-start.7 = (bf16[1,2,72,2048]{3,2,1,0:T(8,128)(2,1)}, bf16[1,2,72,2048]{3,2,1,0:T(8,128)(2,1)S(1)}, u32[]{:S(2)}) copy-start(bf16[1,2,72,2048]{3,2,1,0:T(8,128)(2,1)S(1)} %collective-permute-done.1) | copy-start | bytes 1769476
  44.9 1.1 copy-start.11
  46.1 26.8 %copy-start.5 = (bf16[1,2,72,2048]{3,2,1,0:T(8,128)(2,1)}, bf16[1,2,72,2048]{3,2,1,0:T(8,128)(2,1)S(1)}, u32[]{:S(2)}) copy-start(bf16[1,2,72,2048]{3,2,1,0:T(8,128)(2,1)S(1)} %collective-permute-done.2) | copy-start | bytes 1769476
  72.0 0.8 copy-start.9
  72.9 0.8 copy-start.2
  73.7 122.0 %copy-start.17 = (f32[2,2048]{1,0:T(2,128)S(1)}, f32[2,2048]{1,0:T(2,128)}, u32[]{:S(2)}) copy-start(f32[2,2048]{1,0:T(2,128)} %param.8) | copy-start | bytes 49156
  294.1 0.8 copy-start.13
  303.2 1.3 copy-start.1
  303.2 1.4 copy-start.4
  303.2 1.6 copy-start.12
  303.3 269.0 %all-reduce.13.cloned.1.call-start = ((), (), s32[]{:S(2)}) async-start(), calls=%async_computation.2 | async-start | bytes 524288 | tf_op jit(solution)/shard_map/psum | solution.py:141
  304.8 1.5 copy-start.6
  304.8 1.6 copy-start.8
  304.8 1.6 copy-start.10
  307.8 1.1 copy-start.14
  308.8 407.4 %all-reduce.11.cloned.1.call-start = ((), (), s32[]{:S(2)}) async-start(), calls=%async_computation.1 | async-start | bytes 524288 | tf_op jit(solution)/shard_map/psum | solution.py:108
Sparse Core Ops, SparseCore 0:
  303.4 128.4 reduce-scatter.3
Sparse Core Ops, SparseCore 1:
  308.9 263.3 all-reduce.12
  575.1 141.1 all-reduce.10
where the time goes:
time: 726 us; the launch traced here: 725 us
  waiting for transfers between devices  446 us (61%)
  blocking collectives  215 us (30%)
  between operations  15.8 us (2%)
  starting transfers between devices  15.4 us (2%)
  other arithmetic  13.8 us (2%)
  local copies, waits for them, and re-layouts  13.2 us (2%)
    psum x1, waiting for transfers between devices, body(): grad_pw = lax.psum(snapshot_grad, 'dp')  142 us
    psum x1, waiting for transfers between devices, body(): summed = lax.psum(local_grads, ('dp', 'space'))  136 us
    psum x1, blocking collectives, body(): lax.psum((jnp.sum(input_values, axis=(1, 2, 3)), jnp.sum(input_values * i...  122 us
    unnamed x4, waiting for transfers between devices  121 us
    psum x1, blocking collectives, body(): lax.psum((jnp.sum(normalized_gradient, axis=(1, 2, 3)), jnp.sum(normalize...  93.1 us
    ppermute x4, waiting for transfers between devices, shifted(): lax.ppermute(value, axis, [(source, source + steps) for source in range(l...  45.1 us
    ppermute x4, starting transfers between devices, shifted(): lax.ppermute(value, axis, [(source, source + steps) for source in range(l...  15.3 us
  transfers between devices with their start and end apart: 7, of which 6 were waited for; matrix products, arithmetic and copies ran while one was open for 2% of the time, Pallas kernels for 0%

commit v1 on v0

--- a/solution.py
+++ b/solution.py
@@ -105,7 +105,7 @@
     snapshot_grad = lax.psum_scatter(
         jnp.concatenate(pieces, axis=1), "space", scatter_dimension=0, tiled=True
     )
-    grad_pw = lax.psum(snapshot_grad, "dp")
+    grad_pw = jnp.sum(lax.all_gather(snapshot_grad, "dp"), axis=0)
     grad_used = jnp.stack(
         [
             lax.dot_general(

time: 726 us -> 587 us (0.81)
  the two profiles are of different devices: /device:TPU:2 before, /device:TPU:1 now
where the time goes in v1:
time: 587 us; the launch traced here: 586 us
  waiting for transfers between devices  306 us (52%)
  blocking collectives  214 us (36%)
  starting transfers between devices  16.5 us (3%)
  other arithmetic  16.2 us (3%)
  between operations  15.8 us (3%)
  local copies, waits for them, and re-layouts  9.83 us (2%)
  matrix products  6.94 us (1%)
    psum x1, waiting for transfers between devices, body(): summed = lax.psum(local_grads, ('dp', 'space'))  142 us
    psum x1, blocking collectives, body(): lax.psum((jnp.sum(input_values, axis=(1, 2, 3)), jnp.sum(input_values * i...  120 us
    reduce_scatter x1, waiting for transfers between devices, body(): lax.psum_scatter(jnp.concatenate(pieces, axis=1), 'space', scatter_dimens...  119 us
    psum x1, blocking collectives, body(): lax.psum((jnp.sum(normalized_gradient, axis=(1, 2, 3)), jnp.sum(normalize...  94.3 us
    ppermute x4, waiting for transfers between devices, shifted(): lax.ppermute(value, axis, [(source, source + steps) for source in range(l...  45.5 us
    ppermute x4, starting transfers between devices, shifted(): lax.ppermute(value, axis, [(source, source + steps) for source in range(l...  16.3 us
  transfers between devices with their start and end apart: 7, of which 5 were waited for; matrix products, arithmetic and copies ran while one was open for 2% of the time, Pallas kernels for 0%

profile of v1, /device:TPU:1, one launch (start us, length us, event | category | flops | bytes accessed | tf_op | source)
XLA Modules:
  0.0 585.9 jit_solution(15378630568215255059)
XLA Ops:
  8.1 6.2 %collective-permute-start.2 = (bf16[1,2,72,2048]{3,2,1,0:T(8,128)(2,1)}, bf16[1,2,72,2048]{3,2,1,0:T(8,128)(2,1)S(1)}, u32[]{:S(2)}, u32[]{:S(2)}) collective-permute-start(bf16[1,2,72,2048]{3,2,1,0:T(8,128)(2,1)} %param.5), channel_id=1, source_target_pairs={{0,12},{1,13},{2,14},{3,15},{4,16},{5,17},{6,18},{7,19},{8,20},{9,... | collective-permute-start | bytes 1769480 | tf_op jit(solution)/shard_map/ppermute | solution.py:14
  14.3 1.3 collective-permute-start.1
  15.6 7.5 %collective-permute-start = (bf16[1,2,72,2048]{3,2,1,0:T(8,128)(2,1)}, bf16[1,2,72,2048]{3,2,1,0:T(8,128)(2,1)S(1)}, u32[]{:S(2)}, u32[]{:S(2)}) collective-permute-start(bf16[1,2,72,2048]{3,2,1,0:T(8,128)(2,1)} %param.5), channel_id=1, source_target_pairs={{0,6},{1,7},{2,8},{3,9},{4,10},{5,11},{6,12},{7,13},{8,14},{9,15},... | collective-permute-start | bytes 1769480 | tf_op jit(solution)/shard_map/ppermute | solution.py:14
  23.1 1.3 collective-permute-start.3
  24.5 1.7 convolution_bitcast_fusion
  26.3 0.5 convolution_bitcast_fusion.1
  26.8 7.0 %collective-permute-done.1 = bf16[1,2,72,2048]{3,2,1,0:T(8,128)(2,1)S(1)} collective-permute-done((bf16[1,2,72,2048]{3,2,1,0:T(8,128)(2,1)}, bf16[1,2,72,2048]{3,2,1,0:T(8,128)(2,1)S(1)}, u32[]{:S(2)}, u32[]{:S(2)}) %collective-permute-start.1) | collective-permute-done | bytes 589856 | tf_op jit(solution)/shard_map/ppermute | solution.py:14
  33.8 9.0 %collective-permute-done = bf16[1,2,72,2048]{3,2,1,0:T(8,128)(2,1)S(1)} collective-permute-done((bf16[1,2,72,2048]{3,2,1,0:T(8,128)(2,1)}, bf16[1,2,72,2048]{3,2,1,0:T(8,128)(2,1)S(1)}, u32[]{:S(2)}, u32[]{:S(2)}) %collective-permute-start) | collective-permute-done | bytes 589856 | tf_op jit(solution)/shard_map/ppermute | solution.py:14
  42.8 1.1 fusion.58
  44.0 29.5 %collective-permute-done.3 = bf16[1,2,72,2048]{3,2,1,0:T(8,128)(2,1)S(1)} collective-permute-done((bf16[1,2,72,2048]{3,2,1,0:T(8,128)(2,1)}, bf16[1,2,72,2048]{3,2,1,0:T(8,128)(2,1)S(1)}, u32[]{:S(2)}, u32[]{:S(2)}) %collective-permute-start.3) | collective-permute-done | bytes 589856 | tf_op jit(solution)/shard_map/ppermute | solution.py:14
  73.5 0.8 fusion.57
  74.3 0.8 copy-done.2
  75.2 0.4 convert_reduce_fusion
  75.5 120.0 %all-reduce.7 = (f32[2,2048]{1,0:T(2,128)S(1)}, f32[2,2048]{1,0:T(2,128)S(1)}) all-reduce(f32[2,2048]{1,0:T(2,128)S(1)} %get-tuple-element.39, f32[2,2048]{1,0:T(2,128)S(1)} %get-tuple-element.38), channel_id=1, replica_groups=mesh['dp'=16,'space'=32] {'dp','space'}, use_global_device_ids=true, to_apply=%region_3.4 | all-reduce | flops 8192 | bytes 65536 | tf_op jit(solution)/shard_map/psum | solution.py:77
  195.6 2.0 fusion.61
  197.6 94.3 %all-reduce.6 = (f32[2,2048]{1,0:T(2,128)S(1)}, f32[2,2048]{1,0:T(2,128)S(1)}) all-reduce(f32[2,2048]{1,0:T(2,128)S(1)} %get-tuple-element.10, f32[2,2048]{1,0:T(2,128)S(1)} %get-tuple-element.9), channel_id=1, replica_groups=mesh['dp'=16,'space'=32] {'dp','space'}, use_global_device_ids=true, to_apply=%region_9.10 | all-reduce | flops 8192 | bytes 65536 | tf_op jit(solution)/shard_map/psum | solution.py:122
  291.9 3.2 fusion.10
  295.3 0.5 fusion.64
  296.1 0.5 fusion.63
  296.6 2.5 pad_maximum_fusion
  299.0 5.3 copy.12
  304.5 1.2 copy-done.1
  306.0 1.5 fusion.36
  307.6 1.4 fusion.39
  309.2 0.7 pad_maximum_fusion.2
  310.0 118.7 %reduce-scatter.4.cloned.1.call-done = f32[64,512]{1,0:T(8,128)} async-done(((f32[2048,512]{1,0:T(8,128)}), f32[64,512]{1,0:T(8,128)}) %reduce-scatter.4.cloned.1.call-update) | async-done | bytes 131088 | tf_op jit(solution)/shard_map/reduce_scatter | solution.py:105
  428.8 1.6 fusion.55
  430.4 2.2 fusion.49
  432.6 142.0 %all-reduce.10.cloned.1.call-done = f32[2,9,2048]{2,1,0:T(8,128)} async-done(((f32[2,9,2048]{2,1,0:T(8,128)}), f32[2,9,2048]{2,1,0:T(8,128)}) %all-reduce.10.cloned.1.call-update) | async-done | bytes 147472 | tf_op jit(solution)/shard_map/psum | solution.py:141
  574.6 0.8 constant_dynamic-slice_fusion
  575.4 0.6 copy.11
  576.0 2.4 reduce_sum.209
  (48 shorter events, 1.4 us)
Async XLA Ops:
  8.0 16.5 %copy-start = (bf16[1,2,72,256]{3,2,1,0:T(8,128)(2,1)S(1)}, bf16[1,2,72,256]{3,2,1,0:T(8,128)(2,1)}, u32[]{:S(2)}) copy-start(bf16[1,2,72,256]{3,2,1,0:T(8,128)(2,1)} %param.9) | copy-start | bytes 221188
  8.0 18.2 %copy-start.16 = (bf16[2,9,2048]{2,0,1:T(2,128)(2,1)S(1)}, bf16[2,9,2048]{2,0,1:T(2,128)(2,1)}, u32[]{:S(2)}) copy-start(bf16[2,9,2048]{2,0,1:T(2,128)(2,1)} %param.6) | copy-start | bytes 221188
  8.0 420.7 %reduce-scatter.4.cloned.1.call-start = ((), (), s32[]{:S(2)}) async-start(), calls=%async_computation.3 | async-start | bytes 4325376 | tf_op jit(solution)/shard_map/reduce_scatter | solution.py:105
  8.1 18.2 %copy-start.15 = (bf16[2048,512]{1,0:T(8,128)(2,1)S(1)}, bf16[2048,512]{1,0:T(8,128)(2,1)}, u32[]{:S(2)}) copy-start(bf16[2048,512]{1,0:T(8,128)(2,1)} %param.7) | copy-start | bytes 6291460
  8.1 35.9 %collective-permute-start.2 = (bf16[1,2,72,2048]{3,2,1,0:T(8,128)(2,1)}, bf16[1,2,72,2048]{3,2,1,0:T(8,128)(2,1)S(1)}, u32[]{:S(2)}, u32[]{:S(2)}) collective-permute-start(bf16[1,2,72,2048]{3,2,1,0:T(8,128)(2,1)} %param.5), channel_id=1, source_target_pairs={{0,12},{1,13},{2,14},{3,15},{4,16},{5,17},{6,18},{7,19},{8,20},{9,... | collective-permute-start | bytes 1769480 | tf_op jit(solution)/shard_map/ppermute | solution.py:14
  14.3 19.5 %collective-permute-start.1 = (bf16[1,2,72,2048]{3,2,1,0:T(8,128)(2,1)}, bf16[1,2,72,2048]{3,2,1,0:T(8,128)(2,1)S(1)}, u32[]{:S(2)}, u32[]{:S(2)}) collective-permute-start(bf16[1,2,72,2048]{3,2,1,0:T(8,128)(2,1)} %param.5), channel_id=1, source_target_pairs={{6,0},{7,1},{8,2},{9,3},{10,4},{11,5},{12,6},{13,7},{14,8},{15,9},... | collective-permute-start | bytes 1769480 | tf_op jit(solution)/shard_map/ppermute | solution.py:14
  15.6 27.2 %collective-permute-start = (bf16[1,2,72,2048]{3,2,1,0:T(8,128)(2,1)}, bf16[1,2,72,2048]{3,2,1,0:T(8,128)(2,1)S(1)}, u32[]{:S(2)}, u32[]{:S(2)}) collective-permute-start(bf16[1,2,72,2048]{3,2,1,0:T(8,128)(2,1)} %param.5), channel_id=1, source_target_pairs={{0,6},{1,7},{2,8},{3,9},{4,10},{5,11},{6,12},{7,13},{8,14},{9,15},... | collective-permute-start | bytes 1769480 | tf_op jit(solution)/shard_map/ppermute | solution.py:14
  23.1 50.3 %collective-permute-start.3 = (bf16[1,2,72,2048]{3,2,1,0:T(8,128)(2,1)}, bf16[1,2,72,2048]{3,2,1,0:T(8,128)(2,1)S(1)}, u32[]{:S(2)}, u32[]{:S(2)}) collective-permute-start(bf16[1,2,72,2048]{3,2,1,0:T(8,128)(2,1)} %param.5), channel_id=1, source_target_pairs={{12,0},{13,1},{14,2},{15,3},{16,4},{17,5},{18,6},{19,7},{20,8},{21... | collective-permute-start | bytes 1769480 | tf_op jit(solution)/shard_map/ppermute | solution.py:14
  26.3 16.5 %copy-start.3 = (bf16[1,2,72,2048]{3,2,1,0:T(8,128)(2,1)S(1)}, bf16[1,2,72,2048]{3,2,1,0:T(8,128)(2,1)}, u32[]{:S(2)}) copy-start(bf16[1,2,72,2048]{3,2,1,0:T(8,128)(2,1)} %param.5) | copy-start | bytes 1769476
  33.8 10.1 %copy-start.7 = (bf16[1,2,72,2048]{3,2,1,0:T(8,128)(2,1)}, bf16[1,2,72,2048]{3,2,1,0:T(8,128)(2,1)S(1)}, u32[]{:S(2)}) copy-start(bf16[1,2,72,2048]{3,2,1,0:T(8,128)(2,1)S(1)} %collective-permute-done.1) | copy-start | bytes 1769476
  42.8 1.1 copy-start.11
  44.0 30.4 %copy-start.5 = (bf16[1,2,72,2048]{3,2,1,0:T(8,128)(2,1)}, bf16[1,2,72,2048]{3,2,1,0:T(8,128)(2,1)S(1)}, u32[]{:S(2)}) copy-start(bf16[1,2,72,2048]{3,2,1,0:T(8,128)(2,1)S(1)} %collective-permute-done.2) | copy-start | bytes 1769476
  73.5 0.8 copy-start.9
  74.3 0.8 copy-start.2
  75.2 120.4 %copy-start.17 = (f32[2,2048]{1,0:T(2,128)S(1)}, f32[2,2048]{1,0:T(2,128)}, u32[]{:S(2)}) copy-start(f32[2,2048]{1,0:T(2,128)} %param.8) | copy-start | bytes 49156
  295.3 0.8 copy-start.13
  304.4 1.3 copy-start.1
  304.4 1.4 copy-start.4
  304.4 1.6 copy-start.12
  304.4 270.2 %all-reduce.10.cloned.1.call-start = ((), (), s32[]{:S(2)}) async-start(), calls=%async_computation.1 | async-start | bytes 524288 | tf_op jit(solution)/shard_map/psum | solution.py:141
  306.0 1.5 copy-start.6
  306.0 1.6 copy-start.8
  306.0 1.6 copy-start.10
  309.0 119.8 %copy-start.14 = (bf16[1,1,2,72,2048]{4,3,2,1,0:T(8,128)(2,1)S(1)}, bf16[1,1,2,72,2048]{4,3,2,1,0:T(8,128)(2,1)}, u32[]{:S(2)}) copy-start(bf16[1,1,2,72,2048]{4,3,2,1,0:T(8,128)(2,1)} %copy-done.13) | copy-start | bytes 1769476
  310.0 266.1 %all-gather.3.cloned.1.call-start = ((), (), s32[]{:S(2)}) async-start(), calls=%async_computation.2 | async-start | bytes 2228224 | tf_op jit(solution)/shard_map/all_gather | solution.py:108
Sparse Core Ops, SparseCore 0:
  304.5 124.1 reduce-scatter.3
  430.8 69.7 all-gather.2
Sparse Core Ops, SparseCore 1:
  310.1 264.5 all-reduce.9
